TPU v7x, 32 devices: a whole 2x2x4 slice. The times are simulated.
32 devices in a mesh: dp: 4 (over y, x), seq: 8 (over z, core).
Axes of the slice: x: 2, y: 2, z: 4, core: 2. Of those that a mesh axis runs over, the one named last changes fastest.
Arguments:
- video: bfloat16 [4, 32, 256, 768], P('dp', 'seq'), may hold values from -6 to 6
- space_qkv: bfloat16 [768, 2304], replicated, may hold values from -0.21875 to 0.21875
- space_out: bfloat16 [768, 768], replicated, may hold values from -0.21875 to 0.21875
- time_qkv: bfloat16 [768, 2304], replicated, may hold values from -0.21875 to 0.21875
- time_out: bfloat16 [768, 768], replicated, may hold values from -0.21875 to 0.21875
- proj_weight: bfloat16 [768, 128], replicated, may hold values from -0.21875 to 0.21875
- queries: bfloat16 [32, 32, 128], P('dp'), may hold values from -6 to 6
- query_len: int32 [32], P('dp'), may hold values from 1 to 32, 640 in all
- positive: int32 [32], P('dp'), may hold values from 0 to 3
Outputs:
- video_grad: bfloat16 [4, 32, 256, 128], P('dp', None, 'seq')
- query_grad: bfloat16 [32, 32, 128], P('dp')
- pair_loss: float32 [32, 4], P(None, 'dp')
Inputs may be any that keep to these rules, and one draw needn't show every extreme that they name: `query_len`: the query lengths sum to 5 / 8 of all slots and the longest query fills all 32 slots.
All inputs are finite; a program needn't handle non-finite values. No bound on the sum of `query_len` on one device may be relied on, other than what follows from the above.
Results may differ from a plain program's by a relative error of at most 0.028.
Values may be sent and summed in bfloat16 or wider, within the bound.
A program may use at most 128 MiB of HBM per device.

v0:
```python
import functools

import jax
import jax.numpy as jnp
from jax import lax
from jax.experimental import pallas as pl
from jax.experimental.pallas import tpu as pltpu
from jax.sharding import PartitionSpec as P

HEADS = 12
TEMPER = 0.05
SLOPE = 10.0
OFFSET = -5.0
SHARP = 10.0
CHUNK = 256
PG = 8
F32 = jnp.float32
BF16 = jnp.bfloat16


def dot(a, b):
    return jnp.dot(a, b, preferred_element_type=F32)


def dot_nt(a, b):
    return lax.dot_general(a, b, (((1,), (1,)), ((), ())), preferred_element_type=F32)


def dot_tn(a, b):
    return lax.dot_general(a, b, (((0,), (0,)), ((), ())), preferred_element_type=F32)


def layer_norm(values):
    center = values - jnp.mean(values, axis=-1, keepdims=True)
    spread = jnp.mean(center * center, axis=-1, keepdims=True)
    return (center * lax.rsqrt(spread + 1e-05)).astype(BF16)


def head_unit(values, same_head, scale):
    total = dot((values * values).astype(BF16), same_head)
    return values * (lax.rsqrt(total + 1e-06) * scale)


def blend(qn, kn, v, low, high, mask):
    rows = qn.shape[0]
    lane = lax.broadcasted_iota(jnp.int32, (rows, 128), 1) < 64
    ones = jnp.ones((rows, 128), BF16)
    out = []
    for p in range(CHUNK // 128):
        cols = slice(128 * p, 128 * p + 128)
        kp = kn[:, cols]
        vx = jnp.concatenate([v[:, cols], ones], axis=1)
        res = []
        for half in (low, high):
            e = jnp.exp(dot_nt(qn[:, cols] * half, kp)).astype(BF16)
            if mask is not None:
                e = e * mask
            res.append(dot(e, vx))
        num = jnp.where(lane, res[0][:, :128], res[1][:, :128])
        den = jnp.where(lane, res[0][:, 128:], res[1][:, 128:])
        out.append((num / den).astype(BF16))
    return jnp.concatenate(out, axis=1)


def kernel(
    nd, ns, lq,
    video, w_sq, w_so, w_tq, w_to, w_p, queries, qlen, qpos,
    vg, qg, loss,
    vbuf, sq, so, tq, to, pw, obuf, bl, recv, bl2, mask, kh, ebuf, sums, qs,
    qall, meta, srecv, part, prec, zrec, gath, qht,
    in_sem, w_sem, as_sem, ar_sem, bs_sem, br_sem, qs_sem, qr_sem, ms_sem, mr_sem, ss_sem, sr_sem,
    ps_sem, pr_sem, rs_sem, rr_sem, gs_sem, gr_sem,
):
    frames, patches, width = vbuf.shape
    ploc = patches // ns
    fall = frames * ns
    rows = fall * PG
    groups = ploc // PG
    chunks = width // CHUNK
    qb = qall.shape[1]
    qt = nd * qb
    mrows = qb // 128
    me_d = lax.axis_index("dp")
    me_s = lax.axis_index("seq")

    def ahead(axis, k):
        if axis == "dp":
            return lax.rem(me_d + k, nd)
        peer, bit = 0, 1
        while bit < ns:
            digit = (me_s // bit) % 2
            peer = peer + bit * (1 - digit if k & bit else digit)
            bit *= 2
        return peer

    def remote(src, dst, send, recv_at, axis, peer):
        return pltpu.make_async_remote_copy(
            src_ref=src, dst_ref=dst, send_sem=send, recv_sem=recv_at,
            device_id={axis: peer}, device_id_type=pl.DeviceIdType.MESH,
        )

    pairs = []
    for c in range(chunks):
        for third in range(3):
            cols = pl.ds(third * width + CHUNK * c, CHUNK)
            pairs.append((w_sq.at[:, cols], sq.at[:, cols]))
    first = len(pairs)
    pairs += [(w_so, so), (w_tq, tq), (w_to, to), (w_p, pw)]
    loads = [
        pltpu.make_async_copy(src, dst, w_sem.at[i]) for i, (src, dst) in enumerate(pairs)
    ]

    def frame_load(f):
        return pltpu.make_async_copy(video.at[0, f], vbuf.at[f], in_sem.at[f])

    frame_load(0).start()
    for i in range(first + 1):
        loads[i].start()
    for f in range(1, frames):
        frame_load(f).start()
    for i in range(first + 1, first + 4):
        loads[i].start()

    barrier = pltpu.get_barrier_semaphore()
    for k in range(1, ns):
        pl.semaphore_signal(
            barrier, inc=1, device_id={"seq": ahead("seq", k)},
            device_id_type=pl.DeviceIdType.MESH,
        )
    for k in range(1, nd):
        for c in range(2):
            pl.semaphore_signal(
                barrier, inc=1, device_id={"dp": ahead("dp", k), "seq": ahead("seq", c)},
                device_id_type=pl.DeviceIdType.MESH,
            )

    lane128 = lax.broadcasted_iota(jnp.int32, (1, 128), 1)
    low = (lane128 < 64).astype(F32).astype(BF16)
    high = (lane128 >= 64).astype(F32).astype(BF16)
    ra = lax.broadcasted_iota(jnp.int32, (CHUNK, CHUNK), 0) // 64
    ca = lax.broadcasted_iota(jnp.int32, (CHUNK, CHUNK), 1) // 64
    same_head = (ra == ca).astype(F32).astype(BF16)
    rm = lax.broadcasted_iota(jnp.int32, (rows, rows), 0) % PG
    cm = lax.broadcasted_iota(jnp.int32, (rows, rows), 1) % PG
    mask[...] = (rm == cm).astype(F32).astype(BF16)

    per = 128 // lq
    tile = []
    for source in (qlen, qpos):
        for r in range(mrows):
            row = jnp.zeros((1, 128), jnp.int32)
            for c in range(per):
                row = jnp.where(lane128 // lq == c, source[r * per + c], row)
            tile.append(row)
    tile.append(jnp.zeros((8 - 2 * mrows, 128), jnp.int32))
    meta[me_d] = jnp.concatenate(tile, axis=0)
    qall[me_d] = queries[...]

    pl.semaphore_wait(barrier, 2 * (nd - 1) + ns - 1)

    def query_copy(k):
        return remote(queries, qall.at[me_d], qs_sem.at[k - 1], qr_sem.at[k - 1], "dp", ahead("dp", k))

    def meta_copy(k):
        return remote(meta.at[me_d], meta.at[me_d], ms_sem.at[k - 1], mr_sem.at[k - 1], "dp", ahead("dp", k))

    lead = max(1, groups // 2)
    order = range(ns - 1, 0, -1)

    def rows_copy(f, k):
        peer = ahead("seq", k)
        return remote(
            obuf.at[f, pl.ds(peer * groups, lead)], recv.at[pl.ds(0, lead), me_s, f],
            as_sem.at[f, k - 1], ar_sem.at[f, k - 1], "seq", peer,
        )

    def group_copy(g, k):
        peer = ahead("seq", k)
        return remote(
            obuf.at[:, peer * groups + g], recv.at[g, me_s],
            bs_sem.at[g - lead, k - 1], br_sem.at[g - lead, k - 1], "seq", peer,
        )

    for k in range(1, nd):
        query_copy(k).start()

    def spatial(f, first_time):
        frame_load(f).wait()
        normed = layer_norm(vbuf[f].astype(F32))
        for c in range(chunks):
            at = CHUNK * c
            if first_time:
                for third in range(3):
                    loads[3 * c + third].wait()
            q = dot(normed, sq[:, at:at + CHUNK])
            k = dot(normed, sq[:, width + at:width + at + CHUNK])
            v = dot(normed, sq[:, 2 * width + at:2 * width + at + CHUNK]).astype(BF16)
            qn = head_unit(q, same_head, SHARP).astype(BF16)
            kn = head_unit(k, same_head, 1.0).astype(BF16)
            bl[:, at:at + CHUNK] = blend(qn, kn, v, low, high, None)

    def spatial_out(f):
        for c in range(chunks):
            at = CHUNK * c
            update = dot(bl[...], so[:, at:at + CHUNK])
            obuf[f, :, :, at:at + CHUNK] = (
                vbuf[f, :, at:at + CHUNK].astype(F32) + update
            ).astype(BF16).reshape(patches // PG, PG, CHUNK)
        for k in order:
            rows_copy(f, k).start()

    spatial(0, True)
    loads[first].wait()
    spatial_out(0)
    for k in range(1, nd):
        meta_copy(k).start()

    @pl.loop(1, frames)
    def _(f):
        spatial(f, False)
        spatial_out(f)

    for g in range(lead, groups):
        for k in order:
            group_copy(g, k).start()
    for g in range(groups):
        recv[g, me_s] = obuf[:, me_s * groups + g]

    for k in range(1, nd):
        query_copy(k).wait()
        meta_copy(k).wait()
    for d in range(nd):
        qf = qall[d].astype(F32).T
        norm = lax.rsqrt(jnp.sum(qf * qf, axis=0, keepdims=True) + 1e-06)
        qht[:, d * qb:(d + 1) * qb] = (qf * norm).astype(BF16)
    sums[...] = jnp.zeros_like(sums)
    qs[...] = jnp.zeros_like(qs)
    for i in range(first + 1, first + 4):
        loads[i].wait()
    for f in range(frames):
        for k in order:
            rows_copy(f, k).wait_recv()

    @pl.loop(0, groups)
    def _(g):
        @pl.when(g >= lead)
        def _():
            for k in order:
                group_copy(g, k).wait_recv()

        x = recv[g].astype(F32).reshape(rows, width)
        normed = layer_norm(x)
        for c in range(chunks):
            at = CHUNK * c
            q = dot(normed, tq[:, at:at + CHUNK])
            k = dot(normed, tq[:, width + at:width + at + CHUNK])
            v = dot(normed, tq[:, 2 * width + at:2 * width + at + CHUNK]).astype(BF16)
            qn = head_unit(q, same_head, SHARP).astype(BF16)
            kn = head_unit(k, same_head, 1.0).astype(BF16)
            bl2[:, at:at + CHUNK] = blend(qn, kn, v, low, high, mask[...])
        mixed = x + dot(bl2[...], to[...])
        normed = layer_norm(mixed.astype(BF16).astype(F32))
        proj = dot(normed, pw[...])
        key = (proj * lax.rsqrt(jnp.sum(proj * proj, axis=-1, keepdims=True) + 1e-06)).astype(BF16)
        kh[g] = key
        for c in range(qt // CHUNK):
            cols = slice(CHUNK * c, CHUNK * c + CHUNK)
            e = jnp.exp((dot(key, qht[:, cols]) - 1.0) * (1.0 / TEMPER))
            sums[:, cols] += jnp.sum(e, axis=0, keepdims=True)
            eb = e.astype(BF16)
            ebuf[g, :, cols] = eb
            qs[:, cols] += dot_tn(key, eb)

    for r in range(qt // 128):
        srecv[me_s, r:r + 1, :] = sums[:, 128 * r:128 * r + 128]

    def sums_copy(k):
        return remote(srecv.at[me_s], srecv.at[me_s], ss_sem.at[k - 1], sr_sem.at[k - 1], "seq", ahead("seq", k))

    for k in range(1, ns):
        sums_copy(k).start()
    for k in range(1, ns):
        sums_copy(k).wait()
    total = srecv[0]
    for s in range(1, ns):
        total = total + srecv[s]

    all_len = jnp.concatenate([meta[d, :mrows] for d in range(nd)], axis=0)
    all_pos = jnp.concatenate([meta[d, mrows:2 * mrows] for d in range(nd)], axis=0)
    trows = qt // 128
    slot = lax.broadcasted_iota(jnp.int32, (trows, 128), 1) % lq
    valid = (slot < all_len).astype(F32)
    count = all_len.astype(F32)
    seg_a = lax.broadcasted_iota(jnp.int32, (128, 128), 0) // lq
    seg_b = lax.broadcasted_iota(jnp.int32, (128, 128), 1) // lq
    seg = (seg_a == seg_b).astype(F32)
    smooth = (1.0 + TEMPER * jnp.log(total)) * valid
    score = jnp.dot(smooth, seg, precision=lax.Precision.HIGHEST, preferred_element_type=F32) / count
    sign = jnp.where(all_pos == me_d, 1.0, -1.0)
    margin = sign * (SLOPE * score + OFFSET)
    tail = jnp.exp(-jnp.abs(margin))
    losses = jnp.maximum(-margin, 0.0) + jnp.log1p(tail)
    coeff = -sign * SLOPE / (1.0 + jnp.exp(margin)) * valid / count
    scale = coeff / total
    nq = qt // lq
    qr = lax.broadcasted_iota(jnp.int32, (nq, trows), 0) // per
    qc = lax.broadcasted_iota(jnp.int32, (nq, trows), 1)
    picked = jnp.dot(
        (qr == qc).astype(F32), losses, precision=lax.Precision.HIGHEST, preferred_element_type=F32
    )
    lr = lax.broadcasted_iota(jnp.int32, (nq, 128), 0) % per
    lc = lax.broadcasted_iota(jnp.int32, (nq, 128), 1)
    loss[...] = jnp.sum(jnp.where(lc == lr * lq, picked, 0.0), axis=1, keepdims=True)

    wrow = jnp.concatenate([scale[r:r + 1] for r in range(trows)], axis=1)
    for d in range(nd):
        cols = slice(d * qb, (d + 1) * qb)
        part[d] = (qs[:, cols] * wrow[:, cols]).T.astype(BF16).reshape(2, qb // 2, 128)
    me_c = me_s % 2
    me_z = me_s // 2
    prec[me_d, me_c] = part[me_d, me_c]
    near = [(k, c) for k in range(nd) for c in range(2) if k + c > 0]

    def part_copy(i):
        k, c = near[i]
        peer_d = ahead("dp", k)
        peer_s = ahead("seq", c)
        return pltpu.make_async_remote_copy(
            src_ref=part.at[peer_d, peer_s % 2], dst_ref=prec.at[me_d, me_c],
            send_sem=ps_sem.at[i], recv_sem=pr_sem.at[i],
            device_id={"dp": peer_d, "seq": peer_s}, device_id_type=pl.DeviceIdType.MESH,
        )

    for i in range(len(near)):
        part_copy(i).start()

    wq = (qht[...].astype(F32) * wrow).astype(BF16)
    for b in range(ploc // 16):
        halves = [
            (dot_nt(ebuf[2 * b + h], wq) * float(fall * patches)).reshape(fall, PG, 128)
            for h in range(2)
        ]
        vg[0, :, 16 * b:16 * b + 16, :] = jnp.concatenate(halves, axis=1).astype(BF16)

    for i in range(len(near)):
        part_copy(i).wait()
    acc = jnp.zeros((qb // 2, 128), F32)
    for d in range(nd):
        for c in range(2):
            acc = acc + prec[d, c].astype(F32)
    zrec[me_z] = acc.astype(BF16)

    def chip_copy(k):
        return remote(zrec.at[me_z], zrec.at[me_z], rs_sem.at[k - 1], rr_sem.at[k - 1], "seq", ahead("seq", 2 * k))

    for k in range(ns // 2 - 1, 0, -1):
        chip_copy(k).start()
    for k in range(1, ns // 2):
        chip_copy(k).wait()
    acc = zrec[0].astype(F32)
    for z in range(1, ns // 2):
        acc = acc + zrec[z].astype(F32)
    gath[me_c] = (acc * float(lq)).astype(BF16)
    swap = remote(gath.at[me_c], gath.at[me_c], gs_sem.at[0], gr_sem.at[0], "seq", ahead("seq", 1))
    swap.start()
    swap.wait()
    qg[...] = gath[...].reshape(qg.shape)

    @pl.loop(0, frames)
    def _(f):
        for k in range(1, ns):
            rows_copy(f, k).wait_send()

    for g in range(lead, groups):
        for k in order:
            group_copy(g, k).wait_send()


def finish(vg_in, qg_in, loss_in, vg_out, qg_out, loss_out):
    vg_out[...] = vg_in[...]
    qg_out[...] = qg_in[...]
    loss_out[...] = loss_in[...]


def body(nd, ns, video, space_qkv, space_out, time_qkv, time_out, proj_weight, queries, query_len, positive):
    videos_dev, frames, patches, width = video.shape
    assert videos_dev == 1
    qdev, lq, embed = queries.shape
    ploc = patches // ns
    fall = frames * ns
    rows = fall * PG
    groups = ploc // PG
    qb = qdev * lq
    qt = nd * qb
    vmem = pltpu.VMEM
    dma = pltpu.SemaphoreType.DMA
    anyspec = pl.BlockSpec(memory_space=pl.ANY)
    vspec = pl.BlockSpec(memory_space=pltpu.VMEM)
    sspec = pl.BlockSpec(memory_space=pltpu.SMEM)
    vg, qg, loss = pl.pallas_call(
        functools.partial(kernel, nd, ns, lq),
        out_shape=(
            jax.ShapeDtypeStruct((1, fall, ploc, embed), BF16),
            jax.ShapeDtypeStruct((qdev, lq, embed), BF16),
            jax.ShapeDtypeStruct((nd * qdev, 1), F32),
        ),
        in_specs=[anyspec] * 6 + [vspec, sspec, sspec],
        out_specs=(vspec, vspec, vspec),
        scratch_shapes=[
            vmem((frames, patches, width), BF16),
            vmem(space_qkv.shape, BF16),
            vmem(space_out.shape, BF16),
            vmem(time_qkv.shape, BF16),
            vmem(time_out.shape, BF16),
            vmem(proj_weight.shape, BF16),
            vmem((frames, patches // PG, PG, width), BF16),
            vmem((patches, width), BF16),
            vmem((groups, ns, frames, PG, width), BF16),
            vmem((rows, width), BF16),
            vmem((rows, rows), BF16),
            vmem((groups, rows, embed), BF16),
            vmem((groups, rows, qt), BF16),
            vmem((1, qt), F32),
            vmem((embed, qt), F32),
            vmem((nd, qb, embed), BF16),
            vmem((nd, 8, 128), jnp.int32),
            vmem((ns, qt // 128, 128), F32),
            vmem((nd, 2, qb // 2, embed), BF16),
            vmem((nd, 2, qb // 2, embed), BF16),
            vmem((ns // 2, qb // 2, embed), BF16),
            vmem((2, qb // 2, embed), BF16),
            vmem((embed, qt), BF16),
            dma((frames,)), dma((3 * (width // CHUNK) + 4,)),
            dma((frames, ns - 1)), dma((frames, ns - 1)),
            dma((max(1, groups - groups // 2), ns - 1)), dma((max(1, groups - groups // 2), ns - 1)),
            dma((nd - 1,)), dma((nd - 1,)),
            dma((nd - 1,)), dma((nd - 1,)),
            dma((ns - 1,)), dma((ns - 1,)),
            dma((2 * nd - 1,)), dma((2 * nd - 1,)),
            dma((ns // 2 - 1,)), dma((ns // 2 - 1,)),
            dma((1,)), dma((1,)),
        ],
        compiler_params=pltpu.CompilerParams(
            collective_id=0, has_side_effects=True, vmem_limit_bytes=60 * 1024 * 1024
        ),
    )(
        video, space_qkv, space_out, time_qkv, time_out, proj_weight,
        queries.reshape(qb, embed), query_len, positive,
    )
    vg, qg, loss = pl.pallas_call(
        finish,
        out_shape=(
            jax.ShapeDtypeStruct(vg.shape, BF16),
            jax.ShapeDtypeStruct(qg.shape, BF16),
            jax.ShapeDtypeStruct(loss.shape, F32),
        ),
        in_specs=[vspec] * 3,
        out_specs=(vspec, vspec, vspec),
    )(vg, qg, loss)
    return vg, qg, loss


def solution(mesh):
    nd, ns = mesh.shape["dp"], mesh.shape["seq"]
    placed = (
        P("dp", "seq", None, None),
        P(), P(), P(), P(), P(),
        P("dp", None, None),
        P("dp"),
        P("dp"),
    )
    return jax.shard_map(
        functools.partial(body, nd, ns),
        mesh=mesh,
        in_specs=placed,
        out_specs=(P("dp", None, "seq", None), P("dp", None, None), P(None, "dp")),
        check_vma=False,
    )
```

profile of v0, /device:TPU:0, one launch (start us, length us, event | category | flops | bytes accessed | tf_op | source)
XLA Modules:
  0.0 77.1 jit_solution(10288228300468630102)
XLA Ops:
  0.6 73.4 %shard_map.112 = (bf16[1,32,32,128]{3,2,1,0:T(8,128)(2,1)}, bf16[8,32,128]{2,1,0:T(8,128)(2,1)}, f32[32,1]{1,0:T(8,128)}) custom-call(bf16[1,4,256,768]{3,2,1,0:T(8,128)(2,1)} %video.1, bf16[768,2304]{1,0:T(8,128)(2,1)} %w_sq.1, bf16[768,768]{1,0:T(8,128)(2,1)} %w_so.1, bf16[768,2304]{1,0:T(8,128)(2,1)} %w_tq.1, bf16[768,768]{1,0:T(8,128)(2,1)} %w_to.1, ...), custom_call_target="tpu_custom_call" | custom-call | tf_op jit(solution)/shard_map/pallas_call | solution.py:400
  74.1 1.7 %shard_map.113 = (bf16[1,32,32,128]{3,2,1,0:T(8,128)(2,1)}, bf16[8,32,128]{2,1,0:T(8,128)(2,1)}, f32[32,1]{1,0:T(8,128)}) custom-call(bf16[1,32,32,128]{3,2,1,0:T(8,128)(2,1)} %get-tuple-element.6.vg_in, bf16[8,32,128]{2,1,0:T(8,128)(2,1)} %get-tuple-element.7.qg_in, f32[32,1]{1,0:T(8,128)} %get-tuple-element.8.loss_in), custom_call_target="tpu_custom_call" | custom-call | tf_op jit(solution)/shard_map/pallas_call | solution.py:450
  75.8 1.3 %copy.12 = f32[32,1]{0,1:T(1,128)} copy(f32[32,1]{1,0:T(8,128)} %get-tuple-element.11) | data formatting | bytes 256 | tf_op jit(solution)/shard_map/pallas_call | solution.py:450
where the time goes:
time: 77.3 us; the launch traced here: 77.1 us
  Pallas kernels  75.2 us (97%)
  local copies, waits for them, and re-layouts  1.3 us (2%)
    pallas_call x1, Pallas kernels, body(): pl.pallas_call(functools.partial(kernel, nd, ns, lq), out_shape=(jax.Shap...  73.4 us
    pallas_call x1, Pallas kernels, body(): pl.pallas_call(finish, out_shape=(jax.ShapeDtypeStruct(vg.shape, BF16), j...  1.72 us

commit v1 on v0

--- a/solution.py
+++ b/solution.py
@@ -156,8 +156,6 @@
     meta[me_d] = jnp.concatenate(tile, axis=0)
     qall[me_d] = queries[...]
 
-    pl.semaphore_wait(barrier, 2 * (nd - 1) + ns - 1)
-
     def query_copy(k):
         return remote(queries, qall.at[me_d], qs_sem.at[k - 1], qr_sem.at[k - 1], "dp", ahead("dp", k))
 
@@ -165,7 +163,7 @@
         return remote(meta.at[me_d], meta.at[me_d], ms_sem.at[k - 1], mr_sem.at[k - 1], "dp", ahead("dp", k))
 
     lead = max(1, groups // 2)
-    order = range(ns - 1, 0, -1)
+    order = range(1, ns)
 
     def rows_copy(f, k):
         peer = ahead("seq", k)
@@ -180,9 +178,6 @@
             obuf.at[:, peer * groups + g], recv.at[g, me_s],
             bs_sem.at[g - lead, k - 1], br_sem.at[g - lead, k - 1], "seq", peer,
         )
-
-    for k in range(1, nd):
-        query_copy(k).start()
 
     def spatial(f, first_time):
         frame_load(f).wait()
@@ -211,7 +206,10 @@
 
     spatial(0, True)
     loads[first].wait()
+    pl.semaphore_wait(barrier, 2 * (nd - 1) + ns - 1)
     spatial_out(0)
+    for k in range(1, nd):
+        query_copy(k).start()
     for k in range(1, nd):
         meta_copy(k).start()
 
@@ -303,14 +301,13 @@
     coeff = -sign * SLOPE / (1.0 + jnp.exp(margin)) * valid / count
     scale = coeff / total
     nq = qt // lq
-    qr = lax.broadcasted_iota(jnp.int32, (nq, trows), 0) // per
-    qc = lax.broadcasted_iota(jnp.int32, (nq, trows), 1)
-    picked = jnp.dot(
-        (qr == qc).astype(F32), losses, precision=lax.Precision.HIGHEST, preferred_element_type=F32
-    )
-    lr = lax.broadcasted_iota(jnp.int32, (nq, 128), 0) % per
-    lc = lax.broadcasted_iota(jnp.int32, (nq, 128), 1)
-    loss[...] = jnp.sum(jnp.where(lc == lr * lq, picked, 0.0), axis=1, keepdims=True)
+    lr = lax.broadcasted_iota(jnp.int32, (128, nq), 0)
+    lc = lax.broadcasted_iota(jnp.int32, (128, nq), 1)
+    pick = (lr == lc % per * lq).astype(F32)
+    spread = jnp.dot(losses, pick, precision=lax.Precision.HIGHEST, preferred_element_type=F32)
+    qr = lax.broadcasted_iota(jnp.int32, (trows, nq), 0)
+    qc = lax.broadcasted_iota(jnp.int32, (trows, nq), 1) // per
+    loss[...] = jnp.sum(jnp.where(qr == qc, spread, 0.0), axis=0, keepdims=True)
 
     wrow = jnp.concatenate([scale[r:r + 1] for r in range(trows)], axis=1)
     for d in range(nd):
@@ -402,7 +399,7 @@
         out_shape=(
             jax.ShapeDtypeStruct((1, fall, ploc, embed), BF16),
             jax.ShapeDtypeStruct((qdev, lq, embed), BF16),
-            jax.ShapeDtypeStruct((nd * qdev, 1), F32),
+            jax.ShapeDtypeStruct((1, nd * qdev), F32),
         ),
         in_specs=[anyspec] * 6 + [vspec, sspec, sspec],
         out_specs=(vspec, vspec, vspec),
@@ -457,7 +454,7 @@
         in_specs=[vspec] * 3,
         out_specs=(vspec, vspec, vspec),
     )(vg, qg, loss)
-    return vg, qg, loss
+    return vg, qg, loss.reshape(nd * qdev, 1)
 
 
 def solution(mesh):

time: 77.3 us -> 70.3 us (0.909)
  Pallas kernels: 75.2 us -> 69.5 us
  local copies, waits for them, and re-layouts: 1.3 us -> 0 us
    pallas_call x1, Pallas kernels: 73.4 us -> 67.8 us  [body(): pl.pallas_call(functools.partial(kernel, nd, ns, lq), out_shape=(jax.Shap...]
    pallas_call x1 -> x0, local copies, waits for them, and re-layouts: 1.3 us -> none  [body(): pl.pallas_call(finish, out_shape=(jax.ShapeDtypeStruct(vg.shape, BF16), j...]
where the time goes in v1:
time: 70.3 us; the launch traced here: 70.1 us
  Pallas kernels  69.5 us (99%)
    pallas_call x1, Pallas kernels, body(): pl.pallas_call(functools.partial(kernel, nd, ns, lq), out_shape=(jax.Shap...  67.8 us
    pallas_call x1, Pallas kernels, body(): pl.pallas_call(finish, out_shape=(jax.ShapeDtypeStruct(vg.shape, BF16), j...  1.72 us

profile of v1, /device:TPU:0, one launch (start us, length us, event | category | flops | bytes accessed | tf_op | source)
XLA Modules:
  0.0 70.1 jit_solution(6298478474525461397)
XLA Ops:
  0.6 67.8 %shard_map.112 = (bf16[1,32,32,128]{3,2,1,0:T(8,128)(2,1)}, bf16[8,32,128]{2,1,0:T(8,128)(2,1)}, f32[1,32]{1,0:T(1,128)}) custom-call(bf16[1,4,256,768]{3,2,1,0:T(8,128)(2,1)} %video.1, bf16[768,2304]{1,0:T(8,128)(2,1)} %w_sq.1, bf16[768,768]{1,0:T(8,128)(2,1)} %w_so.1, bf16[768,2304]{1,0:T(8,128)(2,1)} %w_tq.1, bf16[768,768]{1,0:T(8,128)(2,1)} %w_to.1, ...), custom_call_target="tpu_custom_call" | custom-call | tf_op jit(solution)/shard_map/pallas_call | solution.py:397
  68.4 1.7 %shard_map.113 = (bf16[1,32,32,128]{3,2,1,0:T(8,128)(2,1)}, bf16[8,32,128]{2,1,0:T(8,128)(2,1)}, f32[1,32]{1,0:T(1,128)}) custom-call(bf16[1,32,32,128]{3,2,1,0:T(8,128)(2,1)} %get-tuple-element.9.vg_in, bf16[8,32,128]{2,1,0:T(8,128)(2,1)} %get-tuple-element.10.qg_in, f32[1,32]{1,0:T(1,128)} %get-tuple-element.11.loss_in), custom_call_target="tpu_custom_call" | custom-call | tf_op jit(solution)/shard_map/pallas_call | solution.py:447

commit v2 on v1

--- a/solution.py
+++ b/solution.py
@@ -64,12 +64,12 @@
 
 def kernel(
     nd, ns, lq,
-    video, w_sq, w_so, w_tq, w_to, w_p, queries, qlen, qpos,
+    video, w_sq, w_so, w_tq, w_to, w_p, queries, qlen_in, qpos_in,
     vg, qg, loss,
     vbuf, sq, so, tq, to, pw, obuf, bl, recv, bl2, mask, kh, ebuf, sums, qs,
-    qall, meta, srecv, part, prec, zrec, gath, qht,
-    in_sem, w_sem, as_sem, ar_sem, bs_sem, br_sem, qs_sem, qr_sem, ms_sem, mr_sem, ss_sem, sr_sem,
-    ps_sem, pr_sem, rs_sem, rr_sem, gs_sem, gr_sem,
+    qall, meta, srecv, xrecv, part, prec, zrec, gath, qht, vgbuf, qlen, qpos,
+    in_sem, w_sem, q_sem, v_sem, as_sem, ar_sem, bs_sem, br_sem, qs_sem, qr_sem, ms_sem, mr_sem, ss_sem, sr_sem,
+    xs_sem, xr_sem, ps_sem, pr_sem, rs_sem, rr_sem, gs_sem, gr_sem,
 ):
     frames, patches, width = vbuf.shape
     ploc = patches // ns
@@ -113,26 +113,28 @@
     def frame_load(f):
         return pltpu.make_async_copy(video.at[0, f], vbuf.at[f], in_sem.at[f])
 
+    query_loads = [
+        pltpu.make_async_copy(queries, qall.at[me_d], q_sem.at[0]),
+        pltpu.make_async_copy(qlen_in, qlen, q_sem.at[1]),
+        pltpu.make_async_copy(qpos_in, qpos, q_sem.at[2]),
+    ]
     frame_load(0).start()
     for i in range(first + 1):
         loads[i].start()
+    for load in query_loads:
+        load.start()
     for f in range(1, frames):
         frame_load(f).start()
     for i in range(first + 1, first + 4):
         loads[i].start()
 
     barrier = pltpu.get_barrier_semaphore()
-    for k in range(1, ns):
+    others = [(k, c) for k in range(nd) for c in range(ns) if k + c > 0]
+    for k, c in others:
         pl.semaphore_signal(
-            barrier, inc=1, device_id={"seq": ahead("seq", k)},
+            barrier, inc=1, device_id={"dp": ahead("dp", k), "seq": ahead("seq", c)},
             device_id_type=pl.DeviceIdType.MESH,
         )
-    for k in range(1, nd):
-        for c in range(2):
-            pl.semaphore_signal(
-                barrier, inc=1, device_id={"dp": ahead("dp", k), "seq": ahead("seq", c)},
-                device_id_type=pl.DeviceIdType.MESH,
-            )
 
     lane128 = lax.broadcasted_iota(jnp.int32, (1, 128), 1)
     low = (lane128 < 64).astype(F32).astype(BF16)
@@ -144,20 +146,8 @@
     cm = lax.broadcasted_iota(jnp.int32, (rows, rows), 1) % PG
     mask[...] = (rm == cm).astype(F32).astype(BF16)
 
-    per = 128 // lq
-    tile = []
-    for source in (qlen, qpos):
-        for r in range(mrows):
-            row = jnp.zeros((1, 128), jnp.int32)
-            for c in range(per):
-                row = jnp.where(lane128 // lq == c, source[r * per + c], row)
-            tile.append(row)
-    tile.append(jnp.zeros((8 - 2 * mrows, 128), jnp.int32))
-    meta[me_d] = jnp.concatenate(tile, axis=0)
-    qall[me_d] = queries[...]
-
     def query_copy(k):
-        return remote(queries, qall.at[me_d], qs_sem.at[k - 1], qr_sem.at[k - 1], "dp", ahead("dp", k))
+        return remote(qall.at[me_d], qall.at[me_d], qs_sem.at[k - 1], qr_sem.at[k - 1], "dp", ahead("dp", k))
 
     def meta_copy(k):
         return remote(meta.at[me_d], meta.at[me_d], ms_sem.at[k - 1], mr_sem.at[k - 1], "dp", ahead("dp", k))
@@ -206,10 +196,22 @@
 
     spatial(0, True)
     loads[first].wait()
-    pl.semaphore_wait(barrier, 2 * (nd - 1) + ns - 1)
+    pl.semaphore_wait(barrier, nd * ns - 1)
     spatial_out(0)
+    for load in query_loads:
+        load.wait()
     for k in range(1, nd):
         query_copy(k).start()
+    per = 128 // lq
+    tile = []
+    for source in (qlen, qpos):
+        for r in range(mrows):
+            row = jnp.zeros((1, 128), jnp.int32)
+            for c in range(per):
+                row = jnp.where(lane128 // lq == c, source[r * per + c], row)
+            tile.append(row)
+    tile.append(jnp.zeros((8 - 2 * mrows, 128), jnp.int32))
+    meta[me_d] = jnp.concatenate(tile, axis=0)
     for k in range(1, nd):
         meta_copy(k).start()
 
@@ -269,50 +271,31 @@
             ebuf[g, :, cols] = eb
             qs[:, cols] += dot_tn(key, eb)
 
-    for r in range(qt // 128):
-        srecv[me_s, r:r + 1, :] = sums[:, 128 * r:128 * r + 128]
+    for d in range(nd):
+        for r in range(mrows):
+            at = d * qb + 128 * r
+            srecv[me_s, d, r:r + 1, :] = sums[:, at:at + 128]
 
     def sums_copy(k):
         return remote(srecv.at[me_s], srecv.at[me_s], ss_sem.at[k - 1], sr_sem.at[k - 1], "seq", ahead("seq", k))
 
-    for k in range(1, ns):
+    def block_sums_copy(k, c):
+        i = (k - 1) * ns + c
+        peer_d = ahead("dp", k)
+        return pltpu.make_async_remote_copy(
+            src_ref=srecv.at[me_s, peer_d], dst_ref=xrecv.at[me_d, me_s],
+            send_sem=xs_sem.at[i], recv_sem=xr_sem.at[i],
+            device_id={"dp": peer_d, "seq": ahead("seq", c)}, device_id_type=pl.DeviceIdType.MESH,
+        )
+
+    for k in range(ns - 1, 0, -1):
         sums_copy(k).start()
-    for k in range(1, ns):
-        sums_copy(k).wait()
-    total = srecv[0]
-    for s in range(1, ns):
-        total = total + srecv[s]
-
-    all_len = jnp.concatenate([meta[d, :mrows] for d in range(nd)], axis=0)
-    all_pos = jnp.concatenate([meta[d, mrows:2 * mrows] for d in range(nd)], axis=0)
-    trows = qt // 128
-    slot = lax.broadcasted_iota(jnp.int32, (trows, 128), 1) % lq
-    valid = (slot < all_len).astype(F32)
-    count = all_len.astype(F32)
-    seg_a = lax.broadcasted_iota(jnp.int32, (128, 128), 0) // lq
-    seg_b = lax.broadcasted_iota(jnp.int32, (128, 128), 1) // lq
-    seg = (seg_a == seg_b).astype(F32)
-    smooth = (1.0 + TEMPER * jnp.log(total)) * valid
-    score = jnp.dot(smooth, seg, precision=lax.Precision.HIGHEST, preferred_element_type=F32) / count
-    sign = jnp.where(all_pos == me_d, 1.0, -1.0)
-    margin = sign * (SLOPE * score + OFFSET)
-    tail = jnp.exp(-jnp.abs(margin))
-    losses = jnp.maximum(-margin, 0.0) + jnp.log1p(tail)
-    coeff = -sign * SLOPE / (1.0 + jnp.exp(margin)) * valid / count
-    scale = coeff / total
-    nq = qt // lq
-    lr = lax.broadcasted_iota(jnp.int32, (128, nq), 0)
-    lc = lax.broadcasted_iota(jnp.int32, (128, nq), 1)
-    pick = (lr == lc % per * lq).astype(F32)
-    spread = jnp.dot(losses, pick, precision=lax.Precision.HIGHEST, preferred_element_type=F32)
-    qr = lax.broadcasted_iota(jnp.int32, (trows, nq), 0)
-    qc = lax.broadcasted_iota(jnp.int32, (trows, nq), 1) // per
-    loss[...] = jnp.sum(jnp.where(qr == qc, spread, 0.0), axis=0, keepdims=True)
-
-    wrow = jnp.concatenate([scale[r:r + 1] for r in range(trows)], axis=1)
+    for k in range(nd - 1, 0, -1):
+        for c in range(ns - 1, -1, -1):
+            block_sums_copy(k, c).start()
+
     for d in range(nd):
-        cols = slice(d * qb, (d + 1) * qb)
-        part[d] = (qs[:, cols] * wrow[:, cols]).T.astype(BF16).reshape(2, qb // 2, 128)
+        part[d] = qs[:, d * qb:(d + 1) * qb].T.astype(BF16).reshape(2, qb // 2, 128)
     me_c = me_s % 2
     me_z = me_s // 2
     prec[me_d, me_c] = part[me_d, me_c]
@@ -331,27 +314,97 @@
     for i in range(len(near)):
         part_copy(i).start()
 
+    seg_a = lax.broadcasted_iota(jnp.int32, (128, 128), 0) // lq
+    seg_b = lax.broadcasted_iota(jnp.int32, (128, 128), 1) // lq
+    seg = (seg_a == seg_b).astype(F32)
+    slot = lax.broadcasted_iota(jnp.int32, (1, 128), 1) % lq
+
+    def pair_terms(total, lens, hit):
+        valid = (slot < lens).astype(F32)
+        count = lens.astype(F32)
+        smooth = (1.0 + TEMPER * jnp.log(total)) * valid
+        score = jnp.dot(smooth, seg, precision=lax.Precision.HIGHEST, preferred_element_type=F32) / count
+        sign = jnp.where(hit, 1.0, -1.0)
+        margin = sign * (SLOPE * score + OFFSET)
+        coeff = -sign * SLOPE / (1.0 + jnp.exp(margin)) * valid / count
+        return margin, coeff / total
+
+    for k in range(1, ns):
+        sums_copy(k).wait()
+    for k in range(1, nd):
+        for c in range(ns):
+            block_sums_copy(k, c).wait()
+    for s in range(ns):
+        xrecv[me_d, s] = srecv[s, me_d]
+    block_total = []
+    for d in range(nd):
+        total = xrecv[d, 0]
+        for s in range(1, ns):
+            total = total + xrecv[d, s]
+        block_total.append(total)
+    block_total = jnp.concatenate(block_total, axis=0)
+    block_len = jnp.concatenate([meta[me_d, :mrows]] * nd, axis=0)
+    block_pos = jnp.concatenate([meta[me_d, mrows:2 * mrows]] * nd, axis=0)
+    block_video = lax.broadcasted_iota(jnp.int32, (nd * mrows, 128), 0) // mrows
+    _, block_scale = pair_terms(block_total, block_len, block_pos == block_video)
+    half = mrows // 2
+    tall = block_scale.T
+    for i in range(len(near)):
+        part_copy(i).wait()
+    pieces = []
+    for h in range(half):
+        acc = jnp.zeros((128, 128), F32)
+        for d in range(nd):
+            at = d * mrows + h
+            weight = jnp.where(me_c == 0, tall[:, at:at + 1], tall[:, at + half:at + half + 1])
+            both = prec[d, 0, 128 * h:128 * h + 128].astype(F32) + prec[d, 1, 128 * h:128 * h + 128].astype(F32)
+            acc = acc + both * weight
+        pieces.append(acc.astype(BF16))
+    zrec[me_z] = jnp.concatenate(pieces, axis=0)
+
+    def chip_copy(k):
+        return remote(zrec.at[me_z], zrec.at[me_z], rs_sem.at[k - 1], rr_sem.at[k - 1], "seq", ahead("seq", 2 * k))
+
+    for k in range(ns // 2 - 1, 0, -1):
+        chip_copy(k).start()
+
+    trows = qt // 128
+    total = []
+    for d in range(nd):
+        rows_d = srecv[0, d]
+        for s in range(1, ns):
+            rows_d = rows_d + srecv[s, d]
+        total.append(rows_d)
+    total = jnp.concatenate(total, axis=0)
+    all_len = jnp.concatenate([meta[d, :mrows] for d in range(nd)], axis=0)
+    all_pos = jnp.concatenate([meta[d, mrows:2 * mrows] for d in range(nd)], axis=0)
+    margin, scale = pair_terms(total, all_len, all_pos == me_d)
+    wrow = jnp.concatenate([scale[r:r + 1] for r in range(trows)], axis=1)
     wq = (qht[...].astype(F32) * wrow).astype(BF16)
+
+    def grad_out(b):
+        cols = pl.ds(16 * b, 16)
+        return pltpu.make_async_copy(vgbuf.at[0, :, cols, :], vg.at[0, :, cols, :], v_sem.at[b])
+
     for b in range(ploc // 16):
         halves = [
             (dot_nt(ebuf[2 * b + h], wq) * float(fall * patches)).reshape(fall, PG, 128)
             for h in range(2)
         ]
-        vg[0, :, 16 * b:16 * b + 16, :] = jnp.concatenate(halves, axis=1).astype(BF16)
-
-    for i in range(len(near)):
-        part_copy(i).wait()
-    acc = jnp.zeros((qb // 2, 128), F32)
-    for d in range(nd):
-        for c in range(2):
-            acc = acc + prec[d, c].astype(F32)
-    zrec[me_z] = acc.astype(BF16)
-
-    def chip_copy(k):
-        return remote(zrec.at[me_z], zrec.at[me_z], rs_sem.at[k - 1], rr_sem.at[k - 1], "seq", ahead("seq", 2 * k))
-
-    for k in range(ns // 2 - 1, 0, -1):
-        chip_copy(k).start()
+        vgbuf[0, :, 16 * b:16 * b + 16, :] = jnp.concatenate(halves, axis=1).astype(BF16)
+        grad_out(b).start()
+
+    tail = jnp.exp(-jnp.abs(margin))
+    losses = jnp.maximum(-margin, 0.0) + jnp.log1p(tail)
+    nq = qt // lq
+    lr = lax.broadcasted_iota(jnp.int32, (128, nq), 0)
+    lc = lax.broadcasted_iota(jnp.int32, (128, nq), 1)
+    pick = (lr == lc % per * lq).astype(F32)
+    spread = jnp.dot(losses, pick, precision=lax.Precision.HIGHEST, preferred_element_type=F32)
+    qr = lax.broadcasted_iota(jnp.int32, (trows, nq), 0)
+    qc = lax.broadcasted_iota(jnp.int32, (trows, nq), 1) // per
+    loss[...] = jnp.sum(jnp.where(qr == qc, spread, 0.0), axis=0, keepdims=True)
+
     for k in range(1, ns // 2):
         chip_copy(k).wait()
     acc = zrec[0].astype(F32)
@@ -362,6 +415,8 @@
     swap.start()
     swap.wait()
     qg[...] = gath[...].reshape(qg.shape)
+    for b in range(ploc // 16):
+        grad_out(b).wait()
 
     @pl.loop(0, frames)
     def _(f):
@@ -373,10 +428,17 @@
             group_copy(g, k).wait_send()
 
 
-def finish(vg_in, qg_in, loss_in, vg_out, qg_out, loss_out):
-    vg_out[...] = vg_in[...]
-    qg_out[...] = qg_in[...]
-    loss_out[...] = loss_in[...]
+def finish(vg_in, qg_in, loss_in, vg_out, qg_out, loss_out, vg_buf, qg_buf, loss_buf, in_sem, out_sem):
+    steps = ((vg_in, vg_buf, vg_out), (qg_in, qg_buf, qg_out), (loss_in, loss_buf, loss_out))
+    fetch = [pltpu.make_async_copy(a, b, in_sem.at[i]) for i, (a, b, _) in enumerate(steps)]
+    store = [pltpu.make_async_copy(b, c, out_sem.at[i]) for i, (_, b, c) in enumerate(steps)]
+    for copy in fetch:
+        copy.start()
+    for i in range(len(steps)):
+        fetch[i].wait()
+        store[i].start()
+    for copy in store:
+        copy.wait()
 
 
 def body(nd, ns, video, space_qkv, space_out, time_qkv, time_out, proj_weight, queries, query_len, positive):
@@ -393,7 +455,6 @@
     dma = pltpu.SemaphoreType.DMA
     anyspec = pl.BlockSpec(memory_space=pl.ANY)
     vspec = pl.BlockSpec(memory_space=pltpu.VMEM)
-    sspec = pl.BlockSpec(memory_space=pltpu.SMEM)
     vg, qg, loss = pl.pallas_call(
         functools.partial(kernel, nd, ns, lq),
         out_shape=(
@@ -401,8 +462,8 @@
             jax.ShapeDtypeStruct((qdev, lq, embed), BF16),
             jax.ShapeDtypeStruct((1, nd * qdev), F32),
         ),
-        in_specs=[anyspec] * 6 + [vspec, sspec, sspec],
-        out_specs=(vspec, vspec, vspec),
+        in_specs=[anyspec] * 9,
+        out_specs=(anyspec, vspec, vspec),
         scratch_shapes=[
             vmem((frames, patches, width), BF16),
             vmem(space_qkv.shape, BF16),
@@ -421,18 +482,24 @@
             vmem((embed, qt), F32),
             vmem((nd, qb, embed), BF16),
             vmem((nd, 8, 128), jnp.int32),
-            vmem((ns, qt // 128, 128), F32),
+            vmem((ns, nd, qb // 128, 128), F32),
+            vmem((nd, ns, qb // 128, 128), F32),
             vmem((nd, 2, qb // 2, embed), BF16),
             vmem((nd, 2, qb // 2, embed), BF16),
             vmem((ns // 2, qb // 2, embed), BF16),
             vmem((2, qb // 2, embed), BF16),
             vmem((embed, qt), BF16),
+            vmem((1, fall, ploc, embed), BF16),
+            pltpu.SMEM((qdev,), jnp.int32),
+            pltpu.SMEM((qdev,), jnp.int32),
             dma((frames,)), dma((3 * (width // CHUNK) + 4,)),
+            dma((3,)), dma((ploc // 16,)),
             dma((frames, ns - 1)), dma((frames, ns - 1)),
             dma((max(1, groups - groups // 2), ns - 1)), dma((max(1, groups - groups // 2), ns - 1)),
             dma((nd - 1,)), dma((nd - 1,)),
             dma((nd - 1,)), dma((nd - 1,)),
             dma((ns - 1,)), dma((ns - 1,)),
+            dma(((nd - 1) * ns,)), dma(((nd - 1) * ns,)),
             dma((2 * nd - 1,)), dma((2 * nd - 1,)),
             dma((ns // 2 - 1,)), dma((ns // 2 - 1,)),
             dma((1,)), dma((1,)),
@@ -451,8 +518,11 @@
             jax.ShapeDtypeStruct(qg.shape, BF16),
             jax.ShapeDtypeStruct(loss.shape, F32),
         ),
-        in_specs=[vspec] * 3,
-        out_specs=(vspec, vspec, vspec),
+        in_specs=[anyspec] * 3,
+        out_specs=(anyspec, anyspec, anyspec),
+        scratch_shapes=[
+            vmem(vg.shape, BF16), vmem(qg.shape, BF16), vmem(loss.shape, F32), dma((3,)), dma((3,)),
+        ],
     )(vg, qg, loss)
     return vg, qg, loss.reshape(nd * qdev, 1)
 

time: 70.3 us -> 67.4 us (0.959)
  Pallas kernels: 69.5 us -> 66.5 us
    pallas_call x1, Pallas kernels: 67.8 us -> 64.8 us  [body(): pl.pallas_call(functools.partial(kernel, nd, ns, lq), out_shape=(jax.Shap...]
where the time goes in v2:
time: 67.4 us; the launch traced here: 67.3 us
  Pallas kernels  66.5 us (99%)
  between operations  0.8 us (1%)
    pallas_call x1, Pallas kernels, body(): pl.pallas_call(functools.partial(kernel, nd, ns, lq), out_shape=(jax.Shap...  64.8 us
    pallas_call x1, Pallas kernels, body(): pl.pallas_call(finish, out_shape=(jax.ShapeDtypeStruct(vg.shape, BF16), j...  1.72 us

profile of v2, /device:TPU:0, one launch (start us, length us, event | category | flops | bytes accessed | tf_op | source)
XLA Modules:
  0.0 67.3 jit_solution(13767404398663332608)
XLA Ops:
  0.6 64.8 %shard_map.112 = (bf16[1,32,32,128]{3,2,1,0:T(8,128)(2,1)}, bf16[8,32,128]{2,1,0:T(8,128)(2,1)}, f32[1,32]{1,0:T(1,128)}) custom-call(bf16[1,4,256,768]{3,2,1,0:T(8,128)(2,1)} %video.1, bf16[768,2304]{1,0:T(8,128)(2,1)} %w_sq.1, bf16[768,768]{1,0:T(8,128)(2,1)} %w_so.1, bf16[768,2304]{1,0:T(8,128)(2,1)} %w_tq.1, bf16[768,768]{1,0:T(8,128)(2,1)} %w_to.1, ...), custom_call_target="tpu_custom_call" | custom-call | tf_op jit(solution)/shard_map/pallas_call | solution.py:458
  65.4 1.7 %shard_map.113 = (bf16[1,32,32,128]{3,2,1,0:T(8,128)(2,1)}, bf16[8,32,128]{2,1,0:T(8,128)(2,1)}, f32[1,32]{1,0:T(1,128)}) custom-call(bf16[1,32,32,128]{3,2,1,0:T(8,128)(2,1)} %get-tuple-element.9.vg_in, bf16[8,32,128]{2,1,0:T(8,128)(2,1)} %get-tuple-element.10.qg_in, f32[1,32]{1,0:T(1,128)} %get-tuple-element.11.loss_in), custom_call_target="tpu_custom_call" | custom-call | tf_op jit(solution)/shard_map/pallas_call | solution.py:514

commit v3 on v2

--- a/solution.py
+++ b/solution.py
@@ -12,6 +12,7 @@
 SLOPE = 10.0
 OFFSET = -5.0
 SHARP = 10.0
+LOG2E = 1.4426950408889634
 CHUNK = 256
 PG = 8
 F32 = jnp.float32
@@ -41,25 +42,58 @@
     return values * (lax.rsqrt(total + 1e-06) * scale)
 
 
-def blend(qn, kn, v, low, high, mask):
-    rows = qn.shape[0]
+def scores(qn, kn, low, high, mask):
+    out = []
+    for p in range(CHUNK // 128):
+        cols = slice(128 * p, 128 * p + 128)
+        for half in (low, high):
+            e = jnp.exp2(dot_nt(qn[:, cols] * half, kn[:, cols])).astype(BF16)
+            if mask is not None:
+                e = e * mask
+            out.append(e)
+    return out
+
+
+def mix(weights, v):
+    rows = v.shape[0]
     lane = lax.broadcasted_iota(jnp.int32, (rows, 128), 1) < 64
     ones = jnp.ones((rows, 128), BF16)
     out = []
     for p in range(CHUNK // 128):
-        cols = slice(128 * p, 128 * p + 128)
-        kp = kn[:, cols]
-        vx = jnp.concatenate([v[:, cols], ones], axis=1)
-        res = []
-        for half in (low, high):
-            e = jnp.exp(dot_nt(qn[:, cols] * half, kp)).astype(BF16)
-            if mask is not None:
-                e = e * mask
-            res.append(dot(e, vx))
+        vx = jnp.concatenate([v[:, 128 * p:128 * p + 128], ones], axis=1)
+        res = [dot(weights[2 * p + h], vx) for h in range(2)]
         num = jnp.where(lane, res[0][:, :128], res[1][:, :128])
         den = jnp.where(lane, res[0][:, 128:], res[1][:, 128:])
         out.append((num / den).astype(BF16))
     return jnp.concatenate(out, axis=1)
+
+
+def attend(normed, w, same_head, low, high, mask, ready, put):
+    width = normed.shape[1]
+    chunks = width // CHUNK
+
+    def project(c):
+        ready(c)
+        at = CHUNK * c
+        q = dot(normed, w[:, at:at + CHUNK])
+        k = dot(normed, w[:, width + at:width + at + CHUNK])
+        v = dot(normed, w[:, 2 * width + at:2 * width + at + CHUNK]).astype(BF16)
+        return q, k, v
+
+    def unit(q, k):
+        qn = head_unit(q, same_head, SHARP * LOG2E).astype(BF16)
+        return qn, head_unit(k, same_head, 1.0).astype(BF16)
+
+    q, k, v = project(0)
+    qn, kn = unit(q, k)
+    for c in range(chunks):
+        now = v
+        if c + 1 < chunks:
+            q, k, v = project(c + 1)
+        weights = scores(qn, kn, low, high, mask)
+        if c + 1 < chunks:
+            qn, kn = unit(q, k)
+        put(c, mix(weights, now))
 
 
 def kernel(
@@ -172,17 +206,16 @@
     def spatial(f, first_time):
         frame_load(f).wait()
         normed = layer_norm(vbuf[f].astype(F32))
-        for c in range(chunks):
-            at = CHUNK * c
+
+        def ready(c):
             if first_time:
                 for third in range(3):
                     loads[3 * c + third].wait()
-            q = dot(normed, sq[:, at:at + CHUNK])
-            k = dot(normed, sq[:, width + at:width + at + CHUNK])
-            v = dot(normed, sq[:, 2 * width + at:2 * width + at + CHUNK]).astype(BF16)
-            qn = head_unit(q, same_head, SHARP).astype(BF16)
-            kn = head_unit(k, same_head, 1.0).astype(BF16)
-            bl[:, at:at + CHUNK] = blend(qn, kn, v, low, high, None)
+
+        def put(c, value):
+            bl[:, CHUNK * c:CHUNK * c + CHUNK] = value
+
+        attend(normed, sq, same_head, low, high, None, ready, put)
 
     def spatial_out(f):
         for c in range(chunks):
@@ -191,7 +224,7 @@
             obuf[f, :, :, at:at + CHUNK] = (
                 vbuf[f, :, at:at + CHUNK].astype(F32) + update
             ).astype(BF16).reshape(patches // PG, PG, CHUNK)
-        for k in order:
+        for k in reversed(order):
             rows_copy(f, k).start()
 
     spatial(0, True)
@@ -220,9 +253,20 @@
         spatial(f, False)
         spatial_out(f)
 
+    line = me_s // (ns // 4)
+    inner = (line == 1) | (line == 2)
+    late = [k for k in order if k >= ns // 2]
+    soon = [k for k in order if not (k >= ns // 2)]
     for g in range(lead, groups):
-        for k in order:
+        for k in soon:
             group_copy(g, k).start()
+
+    @pl.when(jnp.logical_not(inner))
+    def _():
+        for g in range(lead, groups):
+            for k in late:
+                group_copy(g, k).start()
+
     for g in range(groups):
         recv[g, me_s] = obuf[:, me_s * groups + g]
 
@@ -243,6 +287,11 @@
 
     @pl.loop(0, groups)
     def _(g):
+        @pl.when(jnp.logical_and(inner, jnp.logical_and(g >= 0, g + lead < groups)))
+        def _():
+            for k in late:
+                group_copy(g + lead, k).start()
+
         @pl.when(g >= lead)
         def _():
             for k in order:
@@ -250,26 +299,30 @@
 
         x = recv[g].astype(F32).reshape(rows, width)
         normed = layer_norm(x)
-        for c in range(chunks):
-            at = CHUNK * c
-            q = dot(normed, tq[:, at:at + CHUNK])
-            k = dot(normed, tq[:, width + at:width + at + CHUNK])
-            v = dot(normed, tq[:, 2 * width + at:2 * width + at + CHUNK]).astype(BF16)
-            qn = head_unit(q, same_head, SHARP).astype(BF16)
-            kn = head_unit(k, same_head, 1.0).astype(BF16)
-            bl2[:, at:at + CHUNK] = blend(qn, kn, v, low, high, mask[...])
+
+        def put(c, value):
+            bl2[:, CHUNK * c:CHUNK * c + CHUNK] = value
+
+        attend(normed, tq, same_head, low, high, mask[...], lambda c: None, put)
         mixed = x + dot(bl2[...], to[...])
         normed = layer_norm(mixed.astype(BF16).astype(F32))
         proj = dot(normed, pw[...])
         key = (proj * lax.rsqrt(jnp.sum(proj * proj, axis=-1, keepdims=True) + 1e-06)).astype(BF16)
         kh[g] = key
-        for c in range(qt // CHUNK):
+
+        def similar(c):
             cols = slice(CHUNK * c, CHUNK * c + CHUNK)
-            e = jnp.exp((dot(key, qht[:, cols]) - 1.0) * (1.0 / TEMPER))
+            e = jnp.exp2(dot(key, qht[:, cols]) * (LOG2E / TEMPER) - LOG2E / TEMPER)
             sums[:, cols] += jnp.sum(e, axis=0, keepdims=True)
             eb = e.astype(BF16)
             ebuf[g, :, cols] = eb
-            qs[:, cols] += dot_tn(key, eb)
+            return eb
+
+        eb = similar(0)
+        for c in range(qt // CHUNK):
+            later = similar(c + 1) if c + 1 < qt // CHUNK else None
+            qs[:, CHUNK * c:CHUNK * c + CHUNK] += dot_tn(key, eb)
+            eb = later
 
     for d in range(nd):
         for r in range(mrows):

time: 67.4 us -> 64 us (0.950)
  Pallas kernels: 66.5 us -> 63.2 us
    pallas_call x1, Pallas kernels: 64.8 us -> 61.5 us  [body(): pl.pallas_call(functools.partial(kernel, nd, ns, lq), out_shape=(jax.Shap...]
where the time goes in v3:
time: 64 us; the launch traced here: 63.8 us
  Pallas kernels  63.2 us (99%)
  between operations  0.64 us (1%)
    pallas_call x1, Pallas kernels, body(): pl.pallas_call(functools.partial(kernel, nd, ns, lq), out_shape=(jax.Shap...  61.5 us
    pallas_call x1, Pallas kernels, body(): pl.pallas_call(finish, out_shape=(jax.ShapeDtypeStruct(vg.shape, BF16), j...  1.72 us

profile of v3, /device:TPU:0, one launch (start us, length us, event | category | flops | bytes accessed | tf_op | source)
XLA Modules:
  0.0 63.8 jit_solution(8230580170756348843)
XLA Ops:
  0.6 61.5 %shard_map.112 = (bf16[1,32,32,128]{3,2,1,0:T(8,128)(2,1)}, bf16[8,32,128]{2,1,0:T(8,128)(2,1)}, f32[1,32]{1,0:T(1,128)}) custom-call(bf16[1,4,256,768]{3,2,1,0:T(8,128)(2,1)} %video.1, bf16[768,2304]{1,0:T(8,128)(2,1)} %w_sq.1, bf16[768,768]{1,0:T(8,128)(2,1)} %w_so.1, bf16[768,2304]{1,0:T(8,128)(2,1)} %w_tq.1, bf16[768,768]{1,0:T(8,128)(2,1)} %w_to.1, ...), custom_call_target="tpu_custom_call" | custom-call | tf_op jit(solution)/shard_map/pallas_call | solution.py:511
  62.1 1.7 %shard_map.113 = (bf16[1,32,32,128]{3,2,1,0:T(8,128)(2,1)}, bf16[8,32,128]{2,1,0:T(8,128)(2,1)}, f32[1,32]{1,0:T(1,128)}) custom-call(bf16[1,32,32,128]{3,2,1,0:T(8,128)(2,1)} %get-tuple-element.9.vg_in, bf16[8,32,128]{2,1,0:T(8,128)(2,1)} %get-tuple-element.10.qg_in, f32[1,32]{1,0:T(1,128)} %get-tuple-element.11.loss_in), custom_call_target="tpu_custom_call" | custom-call | tf_op jit(solution)/shard_map/pallas_call | solution.py:567

commit v4 on v3

--- a/solution.py
+++ b/solution.py
@@ -285,8 +285,18 @@
         for k in order:
             rows_copy(f, k).wait_recv()
 
+    def gather_queries(g):
+        key = kh[g]
+        for c in range(qt // CHUNK):
+            cols = slice(CHUNK * c, CHUNK * c + CHUNK)
+            qs[:, cols] += dot_tn(key, ebuf[g, :, cols])
+
     @pl.loop(0, groups)
     def _(g):
+        @pl.when(g > 0)
+        def _():
+            gather_queries(g - 1)
+
         @pl.when(jnp.logical_and(inner, jnp.logical_and(g >= 0, g + lead < groups)))
         def _():
             for k in late:
@@ -310,19 +320,11 @@
         key = (proj * lax.rsqrt(jnp.sum(proj * proj, axis=-1, keepdims=True) + 1e-06)).astype(BF16)
         kh[g] = key
 
-        def similar(c):
+        for c in range(qt // CHUNK):
             cols = slice(CHUNK * c, CHUNK * c + CHUNK)
             e = jnp.exp2(dot(key, qht[:, cols]) * (LOG2E / TEMPER) - LOG2E / TEMPER)
             sums[:, cols] += jnp.sum(e, axis=0, keepdims=True)
-            eb = e.astype(BF16)
-            ebuf[g, :, cols] = eb
-            return eb
-
-        eb = similar(0)
-        for c in range(qt // CHUNK):
-            later = similar(c + 1) if c + 1 < qt // CHUNK else None
-            qs[:, CHUNK * c:CHUNK * c + CHUNK] += dot_tn(key, eb)
-            eb = later
+            ebuf[g, :, cols] = e.astype(BF16)
 
     for d in range(nd):
         for r in range(mrows):
@@ -341,12 +343,13 @@
             device_id={"dp": peer_d, "seq": ahead("seq", c)}, device_id_type=pl.DeviceIdType.MESH,
         )
 
-    for k in range(ns - 1, 0, -1):
-        sums_copy(k).start()
     for k in range(nd - 1, 0, -1):
         for c in range(ns - 1, -1, -1):
             block_sums_copy(k, c).start()
-
+    for k in range(ns - 1, 0, -1):
+        sums_copy(k).start()
+
+    gather_queries(groups - 1)
     for d in range(nd):
         part[d] = qs[:, d * qb:(d + 1) * qb].T.astype(BF16).reshape(2, qb // 2, 128)
     me_c = me_s % 2
@@ -418,7 +421,7 @@
     def chip_copy(k):
         return remote(zrec.at[me_z], zrec.at[me_z], rs_sem.at[k - 1], rr_sem.at[k - 1], "seq", ahead("seq", 2 * k))
 
-    for k in range(ns // 2 - 1, 0, -1):
+    for k in range(1, ns // 2):
         chip_copy(k).start()
 
     trows = qt // 128

time: 64 us -> 63.3 us (0.989)
  Pallas kernels: 63.2 us -> 62.5 us
    pallas_call x1, Pallas kernels: 61.5 us -> 60.8 us  [body(): pl.pallas_call(functools.partial(kernel, nd, ns, lq), out_shape=(jax.Shap...]
where the time goes in v4:
time: 63.3 us; the launch traced here: 63.1 us
  Pallas kernels  62.5 us (99%)
  between operations  0.64 us (1%)
    pallas_call x1, Pallas kernels, body(): pl.pallas_call(functools.partial(kernel, nd, ns, lq), out_shape=(jax.Shap...  60.8 us
    pallas_call x1, Pallas kernels, body(): pl.pallas_call(finish, out_shape=(jax.ShapeDtypeStruct(vg.shape, BF16), j...  1.72 us

profile of v4, /device:TPU:0, one launch (start us, length us, event | category | flops | bytes accessed | tf_op | source)
XLA Modules:
  0.0 63.1 jit_solution(15666758637682974544)
XLA Ops:
  0.6 60.8 %shard_map.112 = (bf16[1,32,32,128]{3,2,1,0:T(8,128)(2,1)}, bf16[8,32,128]{2,1,0:T(8,128)(2,1)}, f32[1,32]{1,0:T(1,128)}) custom-call(bf16[1,4,256,768]{3,2,1,0:T(8,128)(2,1)} %video.1, bf16[768,2304]{1,0:T(8,128)(2,1)} %w_sq.1, bf16[768,768]{1,0:T(8,128)(2,1)} %w_so.1, bf16[768,2304]{1,0:T(8,128)(2,1)} %w_tq.1, bf16[768,768]{1,0:T(8,128)(2,1)} %w_to.1, ...), custom_call_target="tpu_custom_call" | custom-call | tf_op jit(solution)/shard_map/pallas_call | solution.py:514
  61.4 1.7 %shard_map.113 = (bf16[1,32,32,128]{3,2,1,0:T(8,128)(2,1)}, bf16[8,32,128]{2,1,0:T(8,128)(2,1)}, f32[1,32]{1,0:T(1,128)}) custom-call(bf16[1,32,32,128]{3,2,1,0:T(8,128)(2,1)} %get-tuple-element.9.vg_in, bf16[8,32,128]{2,1,0:T(8,128)(2,1)} %get-tuple-element.10.qg_in, f32[1,32]{1,0:T(1,128)} %get-tuple-element.11.loss_in), custom_call_target="tpu_custom_call" | custom-call | tf_op jit(solution)/shard_map/pallas_call | solution.py:570

commit v5 on v4

--- a/solution.py
+++ b/solution.py
@@ -101,8 +101,8 @@
     video, w_sq, w_so, w_tq, w_to, w_p, queries, qlen_in, qpos_in,
     vg, qg, loss,
     vbuf, sq, so, tq, to, pw, obuf, bl, recv, bl2, mask, kh, ebuf, sums, qs,
-    qall, meta, srecv, xrecv, part, prec, zrec, gath, qht, vgbuf, qlen, qpos,
-    in_sem, w_sem, q_sem, v_sem, as_sem, ar_sem, bs_sem, br_sem, qs_sem, qr_sem, ms_sem, mr_sem, ss_sem, sr_sem,
+    qall, meta, srecv, xrecv, part, prec, zrec, gath, qht, vgbuf, lossbuf, qlen, qpos,
+    in_sem, w_sem, q_sem, v_sem, o_sem, as_sem, ar_sem, bs_sem, br_sem, qs_sem, qr_sem, ms_sem, mr_sem, ss_sem, sr_sem,
     xs_sem, xr_sem, ps_sem, pr_sem, rs_sem, rr_sem, gs_sem, gr_sem,
 ):
     frames, patches, width = vbuf.shape
@@ -459,7 +459,9 @@
     spread = jnp.dot(losses, pick, precision=lax.Precision.HIGHEST, preferred_element_type=F32)
     qr = lax.broadcasted_iota(jnp.int32, (trows, nq), 0)
     qc = lax.broadcasted_iota(jnp.int32, (trows, nq), 1) // per
-    loss[...] = jnp.sum(jnp.where(qr == qc, spread, 0.0), axis=0, keepdims=True)
+    lossbuf[...] = jnp.sum(jnp.where(qr == qc, spread, 0.0), axis=0, keepdims=True)
+    loss_out = pltpu.make_async_copy(lossbuf, loss, o_sem.at[0])
+    loss_out.start()
 
     for k in range(1, ns // 2):
         chip_copy(k).wait()
@@ -469,8 +471,13 @@
     gath[me_c] = (acc * float(lq)).astype(BF16)
     swap = remote(gath.at[me_c], gath.at[me_c], gs_sem.at[0], gr_sem.at[0], "seq", ahead("seq", 1))
     swap.start()
+    mine = pltpu.make_async_copy(gath.at[me_c], qg.at[me_c], o_sem.at[1])
+    mine.start()
     swap.wait()
-    qg[...] = gath[...].reshape(qg.shape)
+    other = pltpu.make_async_copy(gath.at[1 - me_c], qg.at[1 - me_c], o_sem.at[2])
+    other.start()
+    loss_out.wait()
+    mine.wait()
     for b in range(ploc // 16):
         grad_out(b).wait()
 
@@ -482,6 +489,7 @@
     for g in range(lead, groups):
         for k in order:
             group_copy(g, k).wait_send()
+    other.wait()
 
 
 def finish(vg_in, qg_in, loss_in, vg_out, qg_out, loss_out, vg_buf, qg_buf, loss_buf, in_sem, out_sem):
@@ -515,11 +523,11 @@
         functools.partial(kernel, nd, ns, lq),
         out_shape=(
             jax.ShapeDtypeStruct((1, fall, ploc, embed), BF16),
-            jax.ShapeDtypeStruct((qdev, lq, embed), BF16),
+            jax.ShapeDtypeStruct((2, qb // 2, embed), BF16),
             jax.ShapeDtypeStruct((1, nd * qdev), F32),
         ),
         in_specs=[anyspec] * 9,
-        out_specs=(anyspec, vspec, vspec),
+        out_specs=(anyspec, anyspec, anyspec),
         scratch_shapes=[
             vmem((frames, patches, width), BF16),
             vmem(space_qkv.shape, BF16),
@@ -546,10 +554,11 @@
             vmem((2, qb // 2, embed), BF16),
             vmem((embed, qt), BF16),
             vmem((1, fall, ploc, embed), BF16),
+            vmem((1, nd * qdev), F32),
             pltpu.SMEM((qdev,), jnp.int32),
             pltpu.SMEM((qdev,), jnp.int32),
             dma((frames,)), dma((3 * (width // CHUNK) + 4,)),
-            dma((3,)), dma((ploc // 16,)),
+            dma((3,)), dma((ploc // 16,)), dma((3,)),
             dma((frames, ns - 1)), dma((frames, ns - 1)),
             dma((max(1, groups - groups // 2), ns - 1)), dma((max(1, groups - groups // 2), ns - 1)),
             dma((nd - 1,)), dma((nd - 1,)),
@@ -580,7 +589,7 @@
             vmem(vg.shape, BF16), vmem(qg.shape, BF16), vmem(loss.shape, F32), dma((3,)), dma((3,)),
         ],
     )(vg, qg, loss)
-    return vg, qg, loss.reshape(nd * qdev, 1)
+    return vg, qg.reshape(qdev, lq, embed), loss.reshape(nd * qdev, 1)
 
 
 def solution(mesh):

time: 63.3 us -> 63.2 us (level)
  no operation moved by 1% of the time
where the time goes in v5:
time: 63.2 us; the launch traced here: 63.1 us
  Pallas kernels  62.4 us (99%)
  between operations  0.64 us (1%)
    pallas_call x1, Pallas kernels, body(): pl.pallas_call(functools.partial(kernel, nd, ns, lq), out_shape=(jax.Shap...  60.7 us
    pallas_call x1, Pallas kernels, body(): pl.pallas_call(finish, out_shape=(jax.ShapeDtypeStruct(vg.shape, BF16), j...  1.72 us

profile of v5, /device:TPU:0, one launch (start us, length us, event | category | flops | bytes accessed | tf_op | source)
XLA Modules:
  0.0 63.1 jit_solution(11994005208339620337)
XLA Ops:
  0.6 60.7 %shard_map.112 = (bf16[1,32,32,128]{3,2,1,0:T(8,128)(2,1)}, bf16[2,128,128]{2,1,0:T(8,128)(2,1)}, f32[1,32]{1,0:T(1,128)}) custom-call(bf16[1,4,256,768]{3,2,1,0:T(8,128)(2,1)} %video.1, bf16[768,2304]{1,0:T(8,128)(2,1)} %w_sq.1, bf16[768,768]{1,0:T(8,128)(2,1)} %w_so.1, bf16[768,2304]{1,0:T(8,128)(2,1)} %w_tq.1, bf16[768,768]{1,0:T(8,128)(2,1)} %w_to.1, ...), custom_call_target="tpu_custom_call" | custom-call | tf_op jit(solution)/shard_map/pallas_call | solution.py:522
  61.3 1.7 %shard_map.113 = (bf16[1,32,32,128]{3,2,1,0:T(8,128)(2,1)}, bf16[2,128,128]{2,1,0:T(8,128)(2,1)}, f32[1,32]{1,0:T(1,128)}) custom-call(bf16[1,32,32,128]{3,2,1,0:T(8,128)(2,1)} %get-tuple-element.9.vg_in, bf16[2,128,128]{2,1,0:T(8,128)(2,1)} %get-tuple-element.10.qg_in, f32[1,32]{1,0:T(1,128)} %get-tuple-element.11.loss_in), custom_call_target="tpu_custom_call" | custom-call | tf_op jit(solution)/shard_map/pallas_call | solution.py:579
